TPU v7x, 32 devices: a whole 2x2x4 slice. The times are simulated.
32 devices in a mesh: user: 4 (over x, core), item: 8 (over z, y).
Axes of the slice: x: 2, y: 2, z: 4, core: 2. Of those that a mesh axis runs over, the one named last changes fastest.
Arguments:
- item_feats: bfloat16 [131072, 1024], P(('user', 'item')), may hold values from -30 to 30
- first_weight: bfloat16 [1024, 512], replicated, may hold values from -0.1875 to 0.1875
- second_weight: bfloat16 [512, 256], replicated, may hold values from -0.25 to 0.25
- counts: int32 [131072], P(('user', 'item')), may hold values from 1 to 245760
- user_embed: bfloat16 [8192, 256], P(('user', 'item')), may hold values from -1 to 1
- list_owner: int32 [4096, 1], P(('user', 'item')), may hold values from 0 to 31, as said below
- list_slot: int32 [4096], P(('user', 'item')), may hold values from 0 to 31
- positive: int32 [8192], P(('user', 'item')), may hold values from 0 to 2047
Outputs:
- user_loss: float32 [8192], P(('user', 'item'))
- user_gradient: float32 [8192, 256], P(('user', 'item'))
- first_gradient: float32 [1024, 512], replicated
- second_gradient: float32 [512, 256], replicated
Inputs may be any that keep to these rules, and one draw needn't show every extreme that they name: `list_owner`: the rows of one device (128 of them, an aligned block) name any one owner at most 8 times; in every draw one owner is named exactly 8 times in the rows of every device.
All inputs are finite; a program needn't handle non-finite values.
Results may differ from a plain program's by a relative error of at most 0.0064.
Values may be sent and summed in bfloat16 or wider, within the bound.
No kernel may reach another device: no remote copies, remote signals or barrier semaphores. Data moves between devices by JAX's collectives and lax.ppermute only.
A program may use at most 192 MiB of HBM per device.

v0:
```python
import jax
import jax.numpy as jnp
from jax import lax
from jax.sharding import PartitionSpec as P

BLK = 128
NQ = 8
QB = 16
LOGIT_SCALE = 20.0
LOSS_SCALE = 4096.0
NORM_EPSILON = 1e-06


def body(
    item_feats, first_weight, second_weight, counts, user_embed, list_owner, list_slot, positive
):
    devices = lax.axis_size(("user", "item"))
    item_rows = item_feats.shape[0]
    own_blocks = item_rows // BLK
    user_rows = user_embed.shape[0]
    requests = list_slot.shape[0]
    capacity = 2 * requests // devices
    group_size = user_rows // NQ
    all_users = user_rows * devices
    linear_one = jnp.dot(item_feats, first_weight, preferred_element_type=jnp.float32)
    hidden = jnp.maximum(linear_one, 0.0).astype(jnp.bfloat16)
    tower_out = jnp.dot(hidden, second_weight, preferred_element_type=jnp.float32)
    item_norm = lax.rsqrt(jnp.sum(tower_out * tower_out, axis=1, keepdims=True) + NORM_EPSILON)
    vector_blocks = (tower_out * item_norm).astype(jnp.bfloat16).reshape(own_blocks, BLK, -1)
    log_blocks = jnp.log(counts.astype(jnp.float32)).astype(jnp.bfloat16).reshape(own_blocks, BLK)
    user_float = user_embed.astype(jnp.float32)
    user_norm = lax.rsqrt(jnp.sum(user_float * user_float, axis=1, keepdims=True) + NORM_EPSILON)
    user_vector = (user_float * user_norm).astype(jnp.bfloat16)
    group_users = user_vector.reshape(NQ, group_size, -1)
    group_pos = positive.reshape(NQ, group_size)
    owners = list_owner[:, 0]
    one_hot = (owners[:, None] == jnp.arange(devices, dtype=jnp.int32)[None, :]).astype(jnp.int32)
    earlier = jnp.cumsum(one_hot, axis=0) - one_hot
    position = owners * capacity + jnp.sum(earlier * one_hot, axis=1)
    send_slots = (
        jnp.zeros((devices * capacity,), jnp.int32)
        .at[position]
        .set(list_slot)
        .reshape(devices, capacity)
    )
    index_rows = jnp.arange(requests, dtype=jnp.int32)
    list_index = index_rows // QB
    offset = index_rows % QB * BLK
    local_pos = group_pos[list_index] - offset[:, None]
    local_pos = jnp.where((local_pos >= 0) & (local_pos < BLK), local_pos, -1)
    slot_users = (
        jnp.zeros((devices * capacity, group_size, group_users.shape[2]), jnp.bfloat16)
        .at[position]
        .set(group_users[list_index])
    )
    slot_pos = jnp.full((devices * capacity, group_size), -1, jnp.int32).at[position].set(local_pos)
    slot_ids, pos_in = (
        lax.all_to_all(send_slots, ("user", "item"), split_axis=0, concat_axis=0, tiled=True),
        lax.all_to_all(
            slot_pos.reshape(devices, capacity, group_size),
            ("user", "item"),
            split_axis=0,
            concat_axis=0,
            tiled=True,
        ),
    )
    users_in = lax.all_to_all(
        slot_users.reshape(devices, capacity, group_size, -1),
        ("user", "item"),
        split_axis=0,
        concat_axis=0,
        tiled=True,
    )
    blocks_in = vector_blocks[slot_ids]
    logs_in = log_blocks[slot_ids].astype(jnp.float32)
    scores = (
        LOGIT_SCALE
        * jnp.einsum("nkue,nkbe->nkub", users_in, blocks_in, preferred_element_type=jnp.float32)
        - logs_in[:, :, None, :]
    )
    exp_scores = jnp.exp(scores)
    is_positive = jnp.arange(BLK, dtype=jnp.int32)[None, None, None, :] == pos_in[:, :, :, None]
    part_totals = jnp.sum(exp_scores, axis=3)
    part_pos = jnp.sum(jnp.where(is_positive, scores, 0.0), axis=3)
    back_totals, back_pos = (
        lax.all_to_all(part_totals, ("user", "item"), split_axis=0, concat_axis=0, tiled=True),
        lax.all_to_all(part_pos, ("user", "item"), split_axis=0, concat_axis=0, tiled=True),
    )
    totals = (
        back_totals.reshape(devices * capacity, group_size)[position]
        .reshape(NQ, QB, group_size)
        .sum(axis=1)
    )
    pos_score = (
        back_pos.reshape(devices * capacity, group_size)[position]
        .reshape(NQ, QB, group_size)
        .sum(axis=1)
    )
    user_loss = jnp.log(totals) - pos_score
    slot_totals = (
        jnp.ones((devices * capacity, group_size), jnp.float32).at[position].set(totals[list_index])
    )
    totals_in = lax.all_to_all(
        slot_totals.reshape(devices, capacity, group_size),
        ("user", "item"),
        split_axis=0,
        concat_axis=0,
        tiled=True,
    )
    score_grad = (
        LOSS_SCALE
        / all_users
        * (exp_scores / totals_in[:, :, :, None] - is_positive.astype(jnp.float32))
    ).astype(jnp.bfloat16)
    returned = (
        LOGIT_SCALE
        * jnp.einsum("nkub,nkue->nkbe", score_grad, users_in, preferred_element_type=jnp.float32)
    ).astype(jnp.bfloat16)
    vector_parts = LOGIT_SCALE * jnp.einsum(
        "nkub,nkbe->nkue", score_grad, blocks_in, preferred_element_type=jnp.float32
    )
    parts_back = lax.all_to_all(
        vector_parts, ("user", "item"), split_axis=0, concat_axis=0, tiled=True
    )
    vector_grad = (
        parts_back.reshape(devices * capacity, group_size, -1)[position]
        .reshape(NQ, QB, group_size, -1)
        .sum(axis=1)
    )
    flat_ids = slot_ids.reshape(-1)
    selector = (jnp.arange(own_blocks, dtype=jnp.int32)[:, None] == flat_ids[None, :]).astype(
        jnp.bfloat16
    )
    item_gradient = jnp.dot(
        selector, returned.reshape(devices * capacity, -1), preferred_element_type=jnp.float32
    ).reshape(item_rows, -1)
    projection = jnp.sum(tower_out * item_gradient, axis=1, keepdims=True)
    out_gradient = (
        item_gradient * item_norm - tower_out * (projection * item_norm * item_norm * item_norm)
    ).astype(jnp.bfloat16)
    second_gradient = jnp.dot(hidden.T, out_gradient, preferred_element_type=jnp.float32)
    act_gradient = jnp.where(
        hidden > 0, jnp.dot(out_gradient, second_weight.T, preferred_element_type=jnp.float32), 0.0
    ).astype(jnp.bfloat16)
    first_gradient = jnp.dot(item_feats.T, act_gradient, preferred_element_type=jnp.float32)
    first_gradient, second_gradient = lax.psum((first_gradient, second_gradient), ("user", "item"))
    vector_grad = vector_grad.reshape(user_rows, -1)
    user_projection = jnp.sum(user_float * vector_grad, axis=1, keepdims=True)
    user_gradient = vector_grad * user_norm - user_float * (
        user_projection * user_norm * user_norm * user_norm
    )
    return (user_loss.reshape(user_rows), user_gradient, first_gradient, second_gradient)


def solution(mesh):
    return jax.shard_map(
        body,
        mesh=mesh,
        in_specs=(
            P(("user", "item"), None),
            P(),
            P(),
            P(("user", "item")),
            P(("user", "item"), None),
            P(("user", "item"), None),
            P(("user", "item")),
            P(("user", "item")),
        ),
        out_specs=(P(("user", "item")), P(("user", "item"), None), P(), P()),
        check_vma=False,
    )
```

profile of v0, /device:TPU:0, one launch (start us, length us, event | category | flops | bytes accessed | tf_op | source)
XLA Modules:
  0.0 490.5 jit_solution(11775205947933808178)
XLA Ops:
  7.2 0.8 fusion.13
  8.0 0.2 reduce_window_sum.11
  8.2 0.8 select_reduce_fusion.1
  9.0 0.7 fusion.27
  9.7 1.1 scatter_custom_fusion.1
  10.8 0.7 all_to_all.27
  11.5 7.3 %all-to-all-start.1 = ((s32[32,1,8]{2,1,0:T(1,128)}), s32[32,1,8]{2,1,0:T(1,128)S(1)}, u32[]{:S(2)}, u32[]{:S(2)}) async-start(s32[32,1,8]{2,1,0:T(1,128)} %bitcast.7), calls=%async_computation.1 | async-start | bytes 32768 | tf_op jit(solution)/shard_map/all_to_all | solution.py:58
  18.8 1.0 fusion.3
  19.9 0.8 reshape.192
  20.6 1.0 scatter_custom_fusion.2
  21.7 0.7 reshape.328
  22.4 3.4 all-to-all-done.1
  25.8 2.6 all-to-all-start.3
  28.4 1.0 fusion.4
  29.4 0.7 gather_fusion
  30.1 2.5 broadcast_in_dim.16
  32.6 15.7 %scatter_fusion = bf16[256,32,256]{2,1,0:T(8,128)(2,1)} fusion(bf16[256,32,256]{2,1,0:T(8,128)(2,1)} %broadcast_in_dim.16, s32[128]{0:T(128)S(1)} %fusion.27, bf16[128,32,256]{2,1,0:T(8,128)(2,1)S(1)} %gather_fusion), kind=kCustom, calls=%fused_computation.8 | custom fusion | bytes 6291968 | tf_op jit(solution)/shard_map/scatter | solution.py:54
  48.3 6.0 %all-to-all-start = ((bf16[32,8,32,256]{3,2,1,0:T(8,128)(2,1)}), bf16[32,8,32,256]{3,2,1,0:T(8,128)(2,1)}, u32[]{:S(2)}, u32[]{:S(2)}) async-start(bf16[32,8,32,256]{3,2,1,0:T(8,128)(2,1)} %bitcast.67), calls=%async_computation | async-start | bytes 8388608 | tf_op jit(solution)/shard_map/all_to_all | solution.py:67
  54.3 8.2 %maximum_convert_fusion = bf16[4096,512]{1,0:T(8,128)(2,1)S(1)} fusion(bf16[4096,1024]{1,0:T(8,128)(2,1)} %param.8, bf16[1024,512]{1,0:T(8,128)(2,1)S(1)} %copy-done), kind=kOutput, calls=%fused_computation.15 | convolution fusion | flops 4299161600 | bytes 13631488 | tf_op jit(solution)/shard_map/dot_general | solution.py:25
  62.5 1.3 multiply_reduce_fusion.1
  63.8 0.7 copy-done.5
  64.6 1.9 copy-done.2
  66.5 0.7 multiply_convert_fusion.2
  67.3 0.9 gather_fusion.2
  68.2 9.4 %gather_fusion.1 = bf16[256,128,256]{2,1,0:T(8,128)(2,1)} fusion(bf16[32,128,256]{2,1,0:T(8,128)(2,1)S(1)} %bitcast.62, s32[1024]{0:T(1024)S(1)} %pad_clamp_fusion.1), kind=kCustom, calls=%fused_computation.1 | custom fusion | bytes 33555456 | tf_op jit(solution)/shard_map/gather | solution.py:74
  77.5 0.5 broadcast.184
  78.1 0.7 reduce.4
  78.9 71.4 %all-to-all-done = bf16[32,8,32,256]{3,2,1,0:T(8,128)(2,1)} async-done(((bf16[32,8,32,256]{3,2,1,0:T(8,128)(2,1)}), bf16[32,8,32,256]{3,2,1,0:T(8,128)(2,1)}, u32[]{:S(2)}, u32[]{:S(2)}) %all-to-all-start) | async-done | bytes 4194336 | tf_op jit(solution)/shard_map/all_to_all | solution.py:67
  150.2 11.4 %exponential_reduce_fusion = (f32[32,8,32]{2,1,0:T(8,128)S(1)}, f32[32,8,32]{2,1,0:T(8,128)S(1)}, f32[32,8,32,128]{3,2,1,0:T(8,128)}) fusion(f32[32,8,128]{2,1,0:T(8,128)S(1)} %bitcast_convert_fusion, s32[32,8,32]{2,1,0:T(8,128)S(1)} %reshape.329, bf16[32,8,32,256]{3,2,1,0:T(8,128)(2,1)} %all-to-all-done, bf16[32,8,128,256]{3,2,1,0:T(8,128)(2,1)} %bitcast.63), kind=kOutput, calls=%fused_computation.26 | convolution fusion | flops 543145984 | bytes 25395200 | tf_op jit(solution)/shard_map/nkue,nkbe->nkub/dot_general | solution.py:78
  161.6 0.7 reshape.330
  162.3 2.6 all-to-all-start.4
  164.9 0.7 reshape.332
  165.7 6.5 %all-to-all-done.4 = f32[32,1,256]{2,1,0:T(1,128)S(1)} async-done(((f32[32,1,256]{2,1,0:T(1,128)}), f32[32,1,256]{2,1,0:T(1,128)S(1)}, u32[]{:S(2)}, u32[]{:S(2)}) %all-to-all-start.4) | async-done | bytes 32800 | tf_op jit(solution)/shard_map/all_to_all | solution.py:87
  172.1 2.7 all-to-all-start.2
  174.9 0.5 broadcast.185
  175.4 0.7 reduce.5
  176.2 5.8 %all-to-all-done.2 = f32[32,1,256]{2,1,0:T(1,128)S(1)} async-done(((f32[32,1,256]{2,1,0:T(1,128)}), f32[32,1,256]{2,1,0:T(1,128)S(1)}, u32[]{:S(2)}, u32[]{:S(2)}) %all-to-all-start.2) | async-done | bytes 32800 | tf_op jit(solution)/shard_map/all_to_all | solution.py:86
  182.0 0.7 reduce.6
  182.9 0.7 gather_fusion.4
  183.5 0.6 gather_fusion.3
  184.2 1.0 scatter_custom_fusion.3
  185.3 8.9 %all_to_all.42 = f32[32,1,256]{2,1,0:T(1,128)S(1)} all-to-all(f32[32,1,256]{2,1,0:T(1,128)S(1)} %reshape.334), channel_id=1, replica_groups=mesh['user'=4,'item'=8] {'user','item'}, dimensions={0} | all-to-all | bytes 65536 | tf_op jit(solution)/shard_map/all_to_all | solution.py:103
  194.2 0.7 reduce.7
  195.0 11.7 %broadcast_multiply_fusion = f32[32,8,32,256]{3,2,1,0:T(8,128)} fusion(bf16[32,8,128,256]{3,2,1,0:T(8,128)(2,1)} %bitcast.64, f32[32,8,32,128]{3,2,1,0:T(8,128)} %get-tuple-element.22, f32[32,8,32]{2,1,0:T(8,128)S(1)} %reshape.335, s32[32,8,32]{2,1,0:T(8,128)S(1)} %reshape.329, f32[32,8,128]{2,1,0:T(8,128)S(1)} %bitcast_convert_fusion), kind=kOutput, calls=%fused_computation.19 | convolution fusion | flops 547356672 | bytes 29556736 | tf_op jit(solution)/shard_map/nkub,nkbe->nkue/dot_general | solution.py:119
  206.7 3.7 all-to-all-start.6
  210.4 0.5 broadcast.183
  210.9 0.7 reduce.3
  211.7 13.0 %fusion = bf16[32,8,128,256]{3,2,1,0:T(8,128)(2,1)} fusion(bf16[32,8,32,256]{3,2,1,0:T(8,128)(2,1)} %all-to-all-done, f32[32,8,32,128]{3,2,1,0:T(8,128)} %get-tuple-element.22, f32[32,8,32]{2,1,0:T(8,128)S(1)} %reshape.335, s32[32,8,32]{2,1,0:T(8,128)S(1)} %reshape.329, f32[32,8,128]{2,1,0:T(8,128)S(1)} %bitcast_convert_fusion), kind=kOutput, calls=%fused_computation.13 | convolution fusion | flops 562036736 | bytes 25362432 | tf_op jit(solution)/shard_map/nkub,nkue->nkbe/dot_general | solution.py:117
  224.7 15.8 %copy.16 = bf16[32,8,128,256]{3,1,2,0:T(8,128)(2,1)S(1)} copy(bf16[32,8,128,256]{3,2,1,0:T(8,128)(2,1)} %fusion) | data formatting | bytes 33554432
  240.5 4.8 fusion.22
  245.3 4.9 reshape.201
  250.2 4.2 multiply_reduce_fusion
  254.4 0.4 copy-done.3
  254.8 1.3 copy-done.4
  256.1 2.4 subtract_convert_fusion
  258.5 2.1 fusion.33
  260.6 11.6 %fusion.2 = f32[1024,512]{0,1:T(8,128)} fusion(bf16[4096,1024]{1,0:T(8,128)(2,1)} %param.8, bf16[4096,512]{1,0:T(8,128)(2,1)} %copy-done.5, bf16[4096,256]{1,0:T(8,128)(2,1)S(1)} %subtract_convert_fusion, bf16[512,256]{1,0:T(8,128)(2,1)S(1)} %copy-done.9), kind=kOutput, calls=%fused_computation.28 | convolution fusion | flops 5375000576 | bytes 17039360 | tf_op jit(solution)/shard_map/dot_general | solution.py:145
  272.2 0.6 sub.52
  272.9 197.3 %all-reduce.3.cloned.1.call-done = (f32[1024,512]{0,1:T(8,128)}, f32[512,256]{1,0:T(8,128)}) async-done(((f32[1024,512]{0,1:T(8,128)}, f32[512,256]{1,0:T(8,128)}), (f32[1024,512]{0,1:T(8,128)}, f32[512,256]{1,0:T(8,128)})) %all-reduce.3.cloned.1.call-update) | async-done | bytes 2621456 | tf_op jit(solution)/shard_map/psum | solution.py:146
  470.2 2.9 copy.15
  473.1 6.2 %gather_fusion.5 = f32[128,32,256]{2,1,0:T(8,128)} fusion(f32[256,32,256]{2,1,0:T(8,128)} %bitcast.18, s32[1024]{0:T(1024)S(1)} %pad_clamp_fusion), kind=kCustom, calls=%fused_computation.7 | custom fusion | bytes 8389120 | tf_op jit(solution)/shard_map/gather | solution.py:126
  479.3 2.6 bitcast_reduce_fusion
  482.0 0.8 fusion.6
  482.9 0.8 copy.20
  (44 shorter events, 1.0 us)
Async XLA Ops:
  7.2 47.1 %copy-start = (bf16[1024,512]{1,0:T(8,128)(2,1)S(1)}, bf16[1024,512]{1,0:T(8,128)(2,1)}, u32[]{:S(2)}) copy-start(bf16[1024,512]{1,0:T(8,128)(2,1)} %param.9) | copy-start | bytes 3145732
  11.5 14.3 %all-to-all-start.1 = ((s32[32,1,8]{2,1,0:T(1,128)}), s32[32,1,8]{2,1,0:T(1,128)S(1)}, u32[]{:S(2)}, u32[]{:S(2)}) async-start(s32[32,1,8]{2,1,0:T(1,128)} %bitcast.7), calls=%async_computation.1 | async-start | bytes 32768 | tf_op jit(solution)/shard_map/all_to_all | solution.py:58
  25.8 22.4 %all-to-all-start.3 = ((s32[32,1,256]{2,1,0:T(1,128)}), s32[32,1,256]{2,1,0:T(1,128)S(1)}, u32[]{:S(2)}, u32[]{:S(2)}) async-start(s32[32,1,256]{2,1,0:T(1,128)} %reshape.328), calls=%async_computation.3 | async-start | bytes 65536 | tf_op jit(solution)/shard_map/all_to_all | solution.py:59
  48.3 6.0 %copy-start.10 = (s32[4096]{0:T(1024)S(1)}, s32[4096]{0:T(1024)}, u32[]{:S(2)}) copy-start(s32[4096]{0:T(1024)} %param.11) | copy-start | bytes 49156
  48.3 102.0 %all-to-all-start = ((bf16[32,8,32,256]{3,2,1,0:T(8,128)(2,1)}), bf16[32,8,32,256]{3,2,1,0:T(8,128)(2,1)}, u32[]{:S(2)}, u32[]{:S(2)}) async-start(bf16[32,8,32,256]{3,2,1,0:T(8,128)(2,1)} %bitcast.67), calls=%async_computation | async-start | bytes 8388608 | tf_op jit(solution)/shard_map/all_to_all | solution.py:67
  54.3 8.2 %copy-start.9 = (bf16[512,256]{1,0:T(8,128)(2,1)S(1)}, bf16[512,256]{1,0:T(8,128)(2,1)}, u32[]{:S(2)}) copy-start(bf16[512,256]{1,0:T(8,128)(2,1)} %param.10) | copy-start | bytes 786436
  62.5 2.0 copy-start.5
  64.5 1.9 copy-start.2
  162.3 9.8 %all-to-all-start.4 = ((f32[32,1,256]{2,1,0:T(1,128)}), f32[32,1,256]{2,1,0:T(1,128)S(1)}, u32[]{:S(2)}, u32[]{:S(2)}) async-start(f32[32,1,256]{2,1,0:T(1,128)} %reshape.330), calls=%async_computation.4 | async-start | bytes 65536 | tf_op jit(solution)/shard_map/all_to_all | solution.py:87
  172.1 9.9 %all-to-all-start.2 = ((f32[32,1,256]{2,1,0:T(1,128)}), f32[32,1,256]{2,1,0:T(1,128)S(1)}, u32[]{:S(2)}, u32[]{:S(2)}) async-start(f32[32,1,256]{2,1,0:T(1,128)} %reshape.332), calls=%async_computation.2 | async-start | bytes 65536 | tf_op jit(solution)/shard_map/all_to_all | solution.py:86
  206.7 266.4 %all-to-all-start.6 = ((f32[32,8,32,256]{3,2,1,0:T(8,128)}), f32[32,8,32,256]{3,2,1,0:T(8,128)}, u32[]{:S(2)}, u32[]{:S(2)}) async-start(f32[32,8,32,256]{3,2,1,0:T(8,128)} %broadcast_multiply_fusion), calls=%async_computation.6 | async-start | bytes 16777216 | tf_op jit(solution)/shard_map/all_to_all | solution.py:122
  210.4 259.8 %all-reduce.3.cloned.1.call-start = ((), (), s32[]{:S(2)}) async-start(), calls=%async_computation.7 | async-start | bytes 5242880 | tf_op jit(solution)/shard_map/psum | solution.py:146
  250.2 4.6 copy-start.3
  250.2 5.9 %copy-start.4 = (f32[4096,256]{1,0:T(8,128)S(1)}, f32[4096,256]{1,0:T(8,128)}, u32[]{:S(2)}) copy-start(f32[4096,256]{1,0:T(8,128)} %reshape.201) | copy-start | bytes 12582916
  256.1 2.4 copy-start.6
  473.1 10.6 %copy-start.1 = (bf16[1024,512]{1,0:T(8,128)(2,1)S(1)}, bf16[1024,512]{1,0:T(8,128)(2,1)}, u32[]{:S(2)}) copy-start(bf16[1024,512]{1,0:T(8,128)(2,1)} %param.9) | copy-start | bytes 3145732
  479.3 2.6 copy-start.7
  479.3 3.6 copy-start.8
Sparse Core Ops, SparseCore 0:
  272.3 197.8 all-reduce.2
where the time goes:
time: 492 us; the launch traced here: 491 us
  waiting for transfers between devices  284 us (58%)
  local copies, waits for them, and re-layouts  73.8 us (15%)
  matrix products  64 us (13%)
  starting transfers between devices  24.9 us (5%)
  other arithmetic  20.1 us (4%)
  between operations  14.4 us (3%)
  blocking collectives  8.88 us (2%)
    psum x1, waiting for transfers between devices, body(): lax.psum((first_gradient, second_gradient), ('user', 'item'))  197 us
    all_to_all x1, waiting for transfers between devices, body(): lax.all_to_all(slot_users.reshape(devices, capacity, group_size, -1), ('u...  71.4 us
    unnamed x33, local copies, waits for them, and re-layouts  26.5 us
    scatter x1, local copies, waits for them, and re-layouts, body(): slot_users = jnp.zeros((devices * capacity, group_size, group_users.shape...  15.7 us
    dot_general x1, matrix products, body(): jnp.einsum('nkub,nkue->nkbe', score_grad, users_in, preferred_element_typ...  13 us
    dot_general x1, matrix products, body(): jnp.einsum('nkub,nkbe->nkue', score_grad, blocks_in, preferred_element_ty...  11.7 us
    dot_general x1, matrix products, body(): jnp.dot(item_feats.T, act_gradient, preferred_element_type=jnp.float32)  11.6 us
    dot_general x1, matrix products, body(): jnp.einsum('nkue,nkbe->nkub', users_in, blocks_in, preferred_element_type...  11.4 us
  transfers between devices with their start and end apart: 7, of which 5 were waited for; matrix products, arithmetic and copies ran while one was open for 23% of the time, Pallas kernels for 0%

commit v1 on v0

--- a/solution.py
+++ b/solution.py
@@ -143,7 +143,9 @@
         hidden > 0, jnp.dot(out_gradient, second_weight.T, preferred_element_type=jnp.float32), 0.0
     ).astype(jnp.bfloat16)
     first_gradient = jnp.dot(item_feats.T, act_gradient, preferred_element_type=jnp.float32)
-    first_gradient, second_gradient = lax.psum((first_gradient, second_gradient), ("user", "item"))
+    first_gradient, second_gradient = lax.psum(
+        lax.psum((first_gradient, second_gradient), "item"), "user"
+    )
     vector_grad = vector_grad.reshape(user_rows, -1)
     user_projection = jnp.sum(user_float * vector_grad, axis=1, keepdims=True)
     user_gradient = vector_grad * user_norm - user_float * (

time: 492 us -> 552 us (1.12)
  waiting for transfers between devices: 284 us -> 344 us
    psum x1 -> x2, waiting for transfers between devices: 197 us -> 257 us  [the longest x1 194 us: body(): lax.psum((first_gradient, second_gradient), 'item')]
  transfers between devices with their start and end apart: 7 -> 8, of which waited for: 5 -> 6; matrix products, arithmetic and copies ran while one was open for 23% -> 20% of each run, Pallas kernels for 0% -> 0%
where the time goes in v1:
time: 552 us; the launch traced here: 550 us
  waiting for transfers between devices  344 us (62%)
  local copies, waits for them, and re-layouts  73.8 us (13%)
  matrix products  64 us (12%)
  starting transfers between devices  24.9 us (5%)
  other arithmetic  20.1 us (4%)
  between operations  14.4 us (3%)
  blocking collectives  8.88 us (2%)
    psum x1, waiting for transfers between devices, body(): lax.psum((first_gradient, second_gradient), 'item')  194 us
    all_to_all x1, waiting for transfers between devices, body(): lax.all_to_all(slot_users.reshape(devices, capacity, group_size, -1), ('u...  71.4 us
    psum x1, waiting for transfers between devices, body(): lax.psum(lax.psum((first_gradient, second_gradient), 'item'), 'user')  62.7 us
    unnamed x33, local copies, waits for them, and re-layouts  26.5 us
    scatter x1, local copies, waits for them, and re-layouts, body(): slot_users = jnp.zeros((devices * capacity, group_size, group_users.shape...  15.7 us
    dot_general x1, matrix products, body(): jnp.einsum('nkub,nkue->nkbe', score_grad, users_in, preferred_element_typ...  13 us
    dot_general x1, matrix products, body(): jnp.einsum('nkub,nkbe->nkue', score_grad, blocks_in, preferred_element_ty...  11.7 us
    dot_general x1, matrix products, body(): jnp.dot(item_feats.T, act_gradient, preferred_element_type=jnp.float32)  11.6 us
  transfers between devices with their start and end apart: 8, of which 6 were waited for; matrix products, arithmetic and copies ran while one was open for 20% of the time, Pallas kernels for 0%

profile of v1, /device:TPU:0, one launch (start us, length us, event | category | flops | bytes accessed | tf_op | source)
XLA Modules:
  0.0 550.4 jit_solution(5154468230276725083)
XLA Ops:
  7.2 0.8 fusion.13
  8.2 0.8 select_reduce_fusion.1
  9.0 0.7 fusion.27
  9.7 1.1 scatter_custom_fusion.1
  10.8 0.7 all_to_all.27
  11.5 7.3 %all-to-all-start.1 = ((s32[32,1,8]{2,1,0:T(1,128)}), s32[32,1,8]{2,1,0:T(1,128)S(1)}, u32[]{:S(2)}, u32[]{:S(2)}) async-start(s32[32,1,8]{2,1,0:T(1,128)} %bitcast.7), calls=%async_computation.1 | async-start | bytes 32768 | tf_op jit(solution)/shard_map/all_to_all | solution.py:58
  18.8 1.0 fusion.3
  19.9 0.8 reshape.192
  20.6 1.0 scatter_custom_fusion.2
  21.7 0.7 reshape.328
  22.4 3.4 all-to-all-done.1
  25.8 2.6 all-to-all-start.3
  28.4 1.0 fusion.4
  29.4 0.7 gather_fusion
  30.1 2.5 broadcast_in_dim.16
  32.6 15.7 %scatter_fusion = bf16[256,32,256]{2,1,0:T(8,128)(2,1)} fusion(bf16[256,32,256]{2,1,0:T(8,128)(2,1)} %broadcast_in_dim.16, s32[128]{0:T(128)S(1)} %fusion.27, bf16[128,32,256]{2,1,0:T(8,128)(2,1)S(1)} %gather_fusion), kind=kCustom, calls=%fused_computation.8 | custom fusion | bytes 6291968 | tf_op jit(solution)/shard_map/scatter | solution.py:54
  48.3 6.0 %all-to-all-start = ((bf16[32,8,32,256]{3,2,1,0:T(8,128)(2,1)}), bf16[32,8,32,256]{3,2,1,0:T(8,128)(2,1)}, u32[]{:S(2)}, u32[]{:S(2)}) async-start(bf16[32,8,32,256]{3,2,1,0:T(8,128)(2,1)} %bitcast.67), calls=%async_computation | async-start | bytes 8388608 | tf_op jit(solution)/shard_map/all_to_all | solution.py:67
  54.3 8.2 %maximum_convert_fusion = bf16[4096,512]{1,0:T(8,128)(2,1)S(1)} fusion(bf16[4096,1024]{1,0:T(8,128)(2,1)} %param.8, bf16[1024,512]{1,0:T(8,128)(2,1)S(1)} %copy-done), kind=kOutput, calls=%fused_computation.15 | convolution fusion | flops 4299161600 | bytes 13631488 | tf_op jit(solution)/shard_map/dot_general | solution.py:25
  62.5 1.3 multiply_reduce_fusion.1
  63.8 0.7 copy-done.5
  64.6 1.9 copy-done.2
  66.5 0.7 multiply_convert_fusion.2
  67.3 0.9 gather_fusion.2
  68.2 9.4 %gather_fusion.1 = bf16[256,128,256]{2,1,0:T(8,128)(2,1)} fusion(bf16[32,128,256]{2,1,0:T(8,128)(2,1)S(1)} %bitcast.62, s32[1024]{0:T(1024)S(1)} %pad_clamp_fusion.1), kind=kCustom, calls=%fused_computation.1 | custom fusion | bytes 33555456 | tf_op jit(solution)/shard_map/gather | solution.py:74
  77.5 0.5 broadcast.184
  78.1 0.7 reduce.4
  78.9 71.4 %all-to-all-done = bf16[32,8,32,256]{3,2,1,0:T(8,128)(2,1)} async-done(((bf16[32,8,32,256]{3,2,1,0:T(8,128)(2,1)}), bf16[32,8,32,256]{3,2,1,0:T(8,128)(2,1)}, u32[]{:S(2)}, u32[]{:S(2)}) %all-to-all-start) | async-done | bytes 4194336 | tf_op jit(solution)/shard_map/all_to_all | solution.py:67
  150.2 11.4 %exponential_reduce_fusion = (f32[32,8,32]{2,1,0:T(8,128)S(1)}, f32[32,8,32]{2,1,0:T(8,128)S(1)}, f32[32,8,32,128]{3,2,1,0:T(8,128)}) fusion(f32[32,8,128]{2,1,0:T(8,128)S(1)} %bitcast_convert_fusion, s32[32,8,32]{2,1,0:T(8,128)S(1)} %reshape.329, bf16[32,8,32,256]{3,2,1,0:T(8,128)(2,1)} %all-to-all-done, bf16[32,8,128,256]{3,2,1,0:T(8,128)(2,1)} %bitcast.63), kind=kOutput, calls=%fused_computation.26 | convolution fusion | flops 543145984 | bytes 25395200 | tf_op jit(solution)/shard_map/nkue,nkbe->nkub/dot_general | solution.py:78
  161.6 0.7 reshape.330
  162.3 2.6 all-to-all-start.4
  164.9 0.7 reshape.332
  165.7 6.5 %all-to-all-done.4 = f32[32,1,256]{2,1,0:T(1,128)S(1)} async-done(((f32[32,1,256]{2,1,0:T(1,128)}), f32[32,1,256]{2,1,0:T(1,128)S(1)}, u32[]{:S(2)}, u32[]{:S(2)}) %all-to-all-start.4) | async-done | bytes 32800 | tf_op jit(solution)/shard_map/all_to_all | solution.py:87
  172.1 2.7 all-to-all-start.2
  174.9 0.5 broadcast.185
  175.4 0.7 reduce.5
  176.2 5.8 %all-to-all-done.2 = f32[32,1,256]{2,1,0:T(1,128)S(1)} async-done(((f32[32,1,256]{2,1,0:T(1,128)}), f32[32,1,256]{2,1,0:T(1,128)S(1)}, u32[]{:S(2)}, u32[]{:S(2)}) %all-to-all-start.2) | async-done | bytes 32800 | tf_op jit(solution)/shard_map/all_to_all | solution.py:86
  182.0 0.7 reduce.6
  182.9 0.7 gather_fusion.4
  183.5 0.6 gather_fusion.3
  184.2 1.0 scatter_custom_fusion.3
  185.3 8.9 %all_to_all.42 = f32[32,1,256]{2,1,0:T(1,128)S(1)} all-to-all(f32[32,1,256]{2,1,0:T(1,128)S(1)} %reshape.334), channel_id=1, replica_groups=mesh['user'=4,'item'=8] {'user','item'}, dimensions={0} | all-to-all | bytes 65536 | tf_op jit(solution)/shard_map/all_to_all | solution.py:103
  194.2 0.7 reduce.7
  195.0 11.7 %broadcast_multiply_fusion = f32[32,8,32,256]{3,2,1,0:T(8,128)} fusion(bf16[32,8,128,256]{3,2,1,0:T(8,128)(2,1)} %bitcast.64, f32[32,8,32,128]{3,2,1,0:T(8,128)} %get-tuple-element.24, f32[32,8,32]{2,1,0:T(8,128)S(1)} %reshape.335, s32[32,8,32]{2,1,0:T(8,128)S(1)} %reshape.329, f32[32,8,128]{2,1,0:T(8,128)S(1)} %bitcast_convert_fusion), kind=kOutput, calls=%fused_computation.19 | convolution fusion | flops 547356672 | bytes 29556736 | tf_op jit(solution)/shard_map/nkub,nkbe->nkue/dot_general | solution.py:119
  206.7 3.7 all-to-all-start.6
  210.4 0.5 broadcast.183
  210.9 0.7 reduce.3
  211.7 13.0 %fusion = bf16[32,8,128,256]{3,2,1,0:T(8,128)(2,1)} fusion(bf16[32,8,32,256]{3,2,1,0:T(8,128)(2,1)} %all-to-all-done, f32[32,8,32,128]{3,2,1,0:T(8,128)} %get-tuple-element.24, f32[32,8,32]{2,1,0:T(8,128)S(1)} %reshape.335, s32[32,8,32]{2,1,0:T(8,128)S(1)} %reshape.329, f32[32,8,128]{2,1,0:T(8,128)S(1)} %bitcast_convert_fusion), kind=kOutput, calls=%fused_computation.13 | convolution fusion | flops 562036736 | bytes 25362432 | tf_op jit(solution)/shard_map/nkub,nkue->nkbe/dot_general | solution.py:117
  224.7 15.8 %copy.16 = bf16[32,8,128,256]{3,1,2,0:T(8,128)(2,1)S(1)} copy(bf16[32,8,128,256]{3,2,1,0:T(8,128)(2,1)} %fusion) | data formatting | bytes 33554432
  240.5 4.8 fusion.22
  245.3 4.9 reshape.201
  250.2 4.2 multiply_reduce_fusion
  254.4 0.4 copy-done.3
  254.8 1.3 copy-done.4
  256.1 2.4 subtract_convert_fusion
  258.5 2.1 fusion.33
  260.6 11.6 %fusion.2 = f32[1024,512]{0,1:T(8,128)} fusion(bf16[4096,1024]{1,0:T(8,128)(2,1)} %param.8, bf16[4096,512]{1,0:T(8,128)(2,1)} %copy-done.5, bf16[4096,256]{1,0:T(8,128)(2,1)S(1)} %subtract_convert_fusion, bf16[512,256]{1,0:T(8,128)(2,1)S(1)} %copy-done.9), kind=kOutput, calls=%fused_computation.28 | convolution fusion | flops 5375000576 | bytes 17039360 | tf_op jit(solution)/shard_map/dot_general | solution.py:145
  272.3 194.4 %all-reduce.5.cloned.1.call-done = (f32[1024,512]{0,1:T(8,128)}, f32[512,256]{1,0:T(8,128)}) async-done(((f32[1024,512]{0,1:T(8,128)}, f32[512,256]{1,0:T(8,128)}), (f32[1024,512]{0,1:T(8,128)}, f32[512,256]{1,0:T(8,128)})) %all-reduce.5.cloned.1.call-update) | async-done | bytes 2621456 | tf_op jit(solution)/shard_map/psum | solution.py:147
  466.7 0.6 sub.52
  467.4 62.7 %all-reduce.7.cloned.1.call-done = (f32[1024,512]{0,1:T(8,128)}, f32[512,256]{1,0:T(8,128)}) async-done(((f32[1024,512]{0,1:T(8,128)}, f32[512,256]{1,0:T(8,128)}), (f32[1024,512]{0,1:T(8,128)}, f32[512,256]{1,0:T(8,128)})) %all-reduce.7.cloned.1.call-update) | async-done | bytes 2621456 | tf_op jit(solution)/shard_map/psum | solution.py:146
  530.1 2.9 copy.15
  533.0 6.2 %gather_fusion.5 = f32[128,32,256]{2,1,0:T(8,128)} fusion(f32[256,32,256]{2,1,0:T(8,128)} %bitcast.18, s32[1024]{0:T(1024)S(1)} %pad_clamp_fusion), kind=kCustom, calls=%fused_computation.7 | custom fusion | bytes 8389120 | tf_op jit(solution)/shard_map/gather | solution.py:126
  539.2 2.6 bitcast_reduce_fusion
  541.9 0.8 fusion.6
  542.8 0.8 copy.22
  (47 shorter events, 1.2 us)
Async XLA Ops:
  7.2 47.1 %copy-start = (bf16[1024,512]{1,0:T(8,128)(2,1)S(1)}, bf16[1024,512]{1,0:T(8,128)(2,1)}, u32[]{:S(2)}) copy-start(bf16[1024,512]{1,0:T(8,128)(2,1)} %param.9) | copy-start | bytes 3145732
  11.5 14.3 %all-to-all-start.1 = ((s32[32,1,8]{2,1,0:T(1,128)}), s32[32,1,8]{2,1,0:T(1,128)S(1)}, u32[]{:S(2)}, u32[]{:S(2)}) async-start(s32[32,1,8]{2,1,0:T(1,128)} %bitcast.7), calls=%async_computation.1 | async-start | bytes 32768 | tf_op jit(solution)/shard_map/all_to_all | solution.py:58
  25.8 22.4 %all-to-all-start.3 = ((s32[32,1,256]{2,1,0:T(1,128)}), s32[32,1,256]{2,1,0:T(1,128)S(1)}, u32[]{:S(2)}, u32[]{:S(2)}) async-start(s32[32,1,256]{2,1,0:T(1,128)} %reshape.328), calls=%async_computation.3 | async-start | bytes 65536 | tf_op jit(solution)/shard_map/all_to_all | solution.py:59
  48.3 6.0 %copy-start.10 = (s32[4096]{0:T(1024)S(1)}, s32[4096]{0:T(1024)}, u32[]{:S(2)}) copy-start(s32[4096]{0:T(1024)} %param.11) | copy-start | bytes 49156
  48.3 102.0 %all-to-all-start = ((bf16[32,8,32,256]{3,2,1,0:T(8,128)(2,1)}), bf16[32,8,32,256]{3,2,1,0:T(8,128)(2,1)}, u32[]{:S(2)}, u32[]{:S(2)}) async-start(bf16[32,8,32,256]{3,2,1,0:T(8,128)(2,1)} %bitcast.67), calls=%async_computation | async-start | bytes 8388608 | tf_op jit(solution)/shard_map/all_to_all | solution.py:67
  54.3 8.2 %copy-start.9 = (bf16[512,256]{1,0:T(8,128)(2,1)S(1)}, bf16[512,256]{1,0:T(8,128)(2,1)}, u32[]{:S(2)}) copy-start(bf16[512,256]{1,0:T(8,128)(2,1)} %param.10) | copy-start | bytes 786436
  62.5 2.0 copy-start.5
  64.5 1.9 copy-start.2
  162.3 9.8 %all-to-all-start.4 = ((f32[32,1,256]{2,1,0:T(1,128)}), f32[32,1,256]{2,1,0:T(1,128)S(1)}, u32[]{:S(2)}, u32[]{:S(2)}) async-start(f32[32,1,256]{2,1,0:T(1,128)} %reshape.330), calls=%async_computation.4 | async-start | bytes 65536 | tf_op jit(solution)/shard_map/all_to_all | solution.py:87
  172.1 9.9 %all-to-all-start.2 = ((f32[32,1,256]{2,1,0:T(1,128)}), f32[32,1,256]{2,1,0:T(1,128)S(1)}, u32[]{:S(2)}, u32[]{:S(2)}) async-start(f32[32,1,256]{2,1,0:T(1,128)} %reshape.332), calls=%async_computation.2 | async-start | bytes 65536 | tf_op jit(solution)/shard_map/all_to_all | solution.py:86
  206.7 326.3 %all-to-all-start.6 = ((f32[32,8,32,256]{3,2,1,0:T(8,128)}), f32[32,8,32,256]{3,2,1,0:T(8,128)}, u32[]{:S(2)}, u32[]{:S(2)}) async-start(f32[32,8,32,256]{3,2,1,0:T(8,128)} %broadcast_multiply_fusion), calls=%async_computation.6 | async-start | bytes 16777216 | tf_op jit(solution)/shard_map/all_to_all | solution.py:122
  210.4 256.3 %all-reduce.5.cloned.1.call-start = ((), (), s32[]{:S(2)}) async-start(), calls=%async_computation.7 | async-start | bytes 5242880 | tf_op jit(solution)/shard_map/psum | solution.py:147
  250.2 4.6 copy-start.3
  250.2 5.9 %copy-start.4 = (f32[4096,256]{1,0:T(8,128)S(1)}, f32[4096,256]{1,0:T(8,128)}, u32[]{:S(2)}) copy-start(f32[4096,256]{1,0:T(8,128)} %reshape.201) | copy-start | bytes 12582916
  256.1 2.4 copy-start.6
  272.2 257.9 %all-reduce.7.cloned.1.call-start = ((), (), s32[]{:S(2)}) async-start(), calls=%async_computation.8 | async-start | bytes 5242880 | tf_op jit(solution)/shard_map/psum | solution.py:146
  533.0 10.6 %copy-start.1 = (bf16[1024,512]{1,0:T(8,128)(2,1)S(1)}, bf16[1024,512]{1,0:T(8,128)(2,1)}, u32[]{:S(2)}) copy-start(bf16[1024,512]{1,0:T(8,128)(2,1)} %param.9) | copy-start | bytes 3145732
  539.2 2.6 copy-start.7
  539.2 3.6 copy-start.8
Sparse Core Ops, SparseCore 0:
  272.3 194.3 all-reduce.4
  469.2 60.8 all-reduce.6
